TPU v7x, 128 devices: a whole 4x4x4 slice. The times are simulated.
128 devices in a mesh: row: 8 (over z, core), col: 16 (over y, x).
Axes of the slice: x: 4, y: 4, z: 4, core: 2. Of those that a mesh axis runs over, the one named last changes fastest.
Arguments:
- tile_values: bfloat16 [8, 16, 512, 128, 128], P('row', 'col'), may hold values from -0.046875 to 0.046875
- tile_rows: int32 [8, 16, 512], P('row', 'col'), may hold values from 0 to 63, as said below
- tile_cols: int32 [8, 16, 512], P('row', 'col'), may hold values from 0 to 31
- tile_count: int32 [8, 16], P('row', 'col'), may hold values from 64 to 512, as said below
- features: bfloat16 [65536, 256], P(('row', 'col')), may hold values from -6 to 6
- weight: bfloat16 [256, 256], replicated, may hold values from -0.375 to 0.375
- cotangent: bfloat16 [65536, 256], P(('row', 'col')), may hold values from -6 to 6
Outputs:
- output: bfloat16 [65536, 256], P(('row', 'col'))
- weight_grad: float32 [256, 256], replicated
- input_grad: float32 [65536, 256], P(('row', 'col'))
Inputs may be any that keep to these rules, and one draw needn't show every extreme that they name: Within a cell, all slots hold distinct positions (tile_rows, tile_cols). `tile_count`: some cell holds exactly 512 tiles in every draw.
All inputs are finite; a program needn't handle non-finite values.
Results may differ from a plain program's by a relative error of at most 0.025.
Values may be sent and summed in bfloat16 or wider, within the bound.
A program may use at most 192 MiB of HBM per device.

v0:
```python
import math
import jax
import jax.numpy as jnp
from jax import lax
from jax.sharding import PartitionSpec as P


def sparse_product(
    tile_block,
    take_index,
    add_index,
    live_count,
    source,
    segments,
    einsum_form,
    loop_count,
    block_size,
):
    tile_edge = tile_block.shape[1]
    feat_width = source.shape[2]
    source_count = source.shape[0]
    source_flat = source.reshape(source_count, tile_edge * feat_width)
    source_ids = lax.iota(jnp.int32, source_count)
    target_ids = lax.iota(jnp.int32, segments)

    def add_block(block_index, running):
        first_slot = block_index * block_size
        tile_part = lax.dynamic_slice_in_dim(tile_block, first_slot, block_size, 0)
        take_part = lax.dynamic_slice_in_dim(take_index, first_slot, block_size, 0)
        add_part = lax.dynamic_slice_in_dim(add_index, first_slot, block_size, 0)
        is_live = first_slot + lax.iota(jnp.int32, block_size) < live_count
        take_table = (take_part[:, None] == source_ids[None, :]).astype(jnp.bfloat16)
        picked = jnp.dot(take_table, source_flat, preferred_element_type=jnp.float32).astype(
            jnp.bfloat16
        )
        picked = picked.reshape(block_size, tile_edge, feat_width)
        products = jnp.einsum(einsum_form, tile_part, picked, preferred_element_type=jnp.float32)
        products = products.reshape(block_size, tile_edge * feat_width)
        upper_part = products.astype(jnp.bfloat16)
        lower_part = (products - upper_part.astype(jnp.float32)).astype(jnp.bfloat16)
        add_table = ((add_part[:, None] == target_ids[None, :]) & is_live[:, None]).astype(
            jnp.bfloat16
        )
        contract = (((0,), (0,)), ((), ()))
        added = lax.dot_general(add_table, upper_part, contract, preferred_element_type=jnp.float32)
        added = added + lax.dot_general(
            add_table, lower_part, contract, preferred_element_type=jnp.float32
        )
        return running + added

    initial = jnp.zeros((segments, tile_edge * feat_width), jnp.float32)
    summed = lax.fori_loop(0, loop_count, add_block, initial)
    return summed.reshape(segments, tile_edge, feat_width)


def activation(aggregated, weight, cot_rows):
    hidden = jnp.dot(aggregated, weight, preferred_element_type=jnp.float32)
    sigmoid_value = jax.nn.sigmoid(hidden)
    output = (hidden * sigmoid_value).astype(jnp.bfloat16)
    silu_slope = sigmoid_value * (1.0 + hidden * (1.0 - sigmoid_value))
    hidden_grad = (cot_rows.astype(jnp.float32) * silu_slope).astype(jnp.bfloat16)
    return (output, hidden_grad)


def per_device(tile_values, tile_rows, tile_cols, tile_count, features, weight, cotangent):
    slot_total = tile_values.shape[2]
    tile_edge = tile_values.shape[3]
    tile_block = tile_values.reshape(slot_total, tile_edge, tile_edge)
    row_index = tile_rows.reshape(slot_total)
    col_index = tile_cols.reshape(slot_total)
    live_count = tile_count.reshape(())
    own_rows = features.shape[0]
    feat_width = features.shape[1]
    row_count = lax.axis_size("row")
    col_count = lax.axis_size("col")
    row_tiles = col_count * own_rows // tile_edge
    col_tiles = row_count * own_rows // tile_edge
    block_size = min(slot_total, 64)
    loop_count = slot_total // block_size
    column_block = lax.all_gather(features, "row", axis=0, tiled=True)
    source = column_block.reshape(col_tiles, tile_edge, feat_width)
    partial_rows = sparse_product(
        tile_block,
        col_index,
        row_index,
        live_count,
        source,
        row_tiles,
        "kab,kbf->kaf",
        loop_count,
        block_size,
    )
    partial_flat = partial_rows.reshape(row_tiles * tile_edge, feat_width)
    node_total = row_count * col_count * own_rows
    aggregated = lax.psum_scatter(
        partial_flat.astype(jnp.bfloat16), "col", scatter_dimension=0, tiled=True
    )
    output, hidden_grad = activation(aggregated, weight, cotangent)
    own_grad = lax.dot_general(
        hidden_grad, weight, (((1,), (1,)), ((), ())), preferred_element_type=jnp.float32
    ).astype(jnp.bfloat16)
    row_block = lax.all_gather(own_grad, "col", axis=0, tiled=True)
    local_grad = lax.dot_general(
        aggregated, hidden_grad, (((0,), (0,)), ((), ())), preferred_element_type=jnp.float32
    )
    weight_grad = lax.psum(local_grad, ("row", "col")) * (1.0 / math.sqrt(node_total))
    source_back = row_block.reshape(row_tiles, tile_edge, feat_width)
    partial_cols = sparse_product(
        tile_block,
        row_index,
        col_index,
        live_count,
        source_back,
        col_tiles,
        "kab,kaf->kbf",
        loop_count,
        block_size,
    )
    input_grad = lax.psum_scatter(
        partial_cols.reshape(col_tiles * tile_edge, feat_width).astype(jnp.bfloat16),
        "row",
        scatter_dimension=0,
        tiled=True,
    ).astype(jnp.float32)
    return (output, weight_grad, input_grad)


def solution(mesh):
    placed = (
        P("row", "col", None, None, None),
        P("row", "col", None),
        P("row", "col", None),
        P("row", "col"),
        P(("row", "col"), None),
        P(),
        P(("row", "col"), None),
    )
    return jax.shard_map(
        per_device,
        mesh=mesh,
        in_specs=placed,
        out_specs=(P(("row", "col"), None), P(), P(("row", "col"), None)),
        check_vma=False,
    )
```

profile of v0, /device:TPU:0, one launch (start us, length us, event | category | flops | bytes accessed | tf_op | source)
XLA Modules:
  0.0 546.3 jit_solution(16715004213160616526)
XLA Ops:
  8.0 29.6 %all-gather.3.cloned.1.call-done = bf16[4096,256]{1,0:T(8,128)(2,1)} async-done(((bf16[512,256]{1,0:T(8,128)(2,1)}), bf16[4096,256]{1,0:T(8,128)(2,1)}) %all-gather.3.cloned.1.call-update) | async-done | bytes 2097168 | tf_op jit(solution)/shard_map/all_gather | solution.py:80
  37.6 2.9 reshape_reshape.8
  40.5 148.5 %while.28 = (s32[]{:T(128)}, f32[64,32768]{1,0:T(8,128)}, s32[512]{0:T(512)S(1)}, s32[]{:T(128)}, bf16[512,128,128]{2,1,0:T(8,128)(2,1)}, /*index=5*/s32[512]{0:...) while((s32[]{:T(128)}, f32[64,32768]{1,0:T(8,128)}, ...), condition=%wide.region_1.0_spmd.clone, body=%wide.region_0.0_spmd.clone.sunk | while | flops 1226852480 | bytes 96471168 | solution.py:52
  43.8 2.9 fusion.73
  46.6 4.7 copy.22
  52.7 4.5 fusion.75
  60.4 2.9 fusion.73
  63.3 4.7 copy.22
  69.4 6.7 %fusion.75 = f32[64,32768]{1,0:T(8,128)} fusion(f32[64,32768]{1,0:T(8,128)S(1)} %fusion.74, f32[64,32768]{1,0:T(8,128)} %get-tuple-element.504, f32[64,32768]{1,0:T(8,128)S(1)} %bitcast.50, pred[]{:T(512)S(6)} %compare.6, s32[64]{0:T(128)S(1)} %dynamic_slice.60, pred[64]{0:T(512)(128)(4,1)S(1)} %add_compare_fusion.4), kind=kOutput, calls=%fused_computation.5.clone.1 | convolution fusion | flops 283123712 | bytes 33554752 | tf_op jit(solution)/shard_map/while/body/eval_jaxpr/dot_general | solution.py:46
  79.3 2.9 fusion.73
  82.1 4.7 copy.22
  88.2 6.7 %fusion.75 = f32[64,32768]{1,0:T(8,128)} fusion(f32[64,32768]{1,0:T(8,128)S(1)} %fusion.74, f32[64,32768]{1,0:T(8,128)} %get-tuple-element.504, f32[64,32768]{1,0:T(8,128)S(1)} %bitcast.50, pred[]{:T(512)S(6)} %compare.6, s32[64]{0:T(128)S(1)} %dynamic_slice.60, pred[64]{0:T(512)(128)(4,1)S(1)} %add_compare_fusion.4), kind=kOutput, calls=%fused_computation.5.clone.1 | convolution fusion | flops 283123712 | bytes 33554752 | tf_op jit(solution)/shard_map/while/body/eval_jaxpr/dot_general | solution.py:46
  98.1 2.9 fusion.73
  100.9 4.7 copy.22
  107.1 6.7 %fusion.75 = f32[64,32768]{1,0:T(8,128)} fusion(f32[64,32768]{1,0:T(8,128)S(1)} %fusion.74, f32[64,32768]{1,0:T(8,128)} %get-tuple-element.504, f32[64,32768]{1,0:T(8,128)S(1)} %bitcast.50, pred[]{:T(512)S(6)} %compare.6, s32[64]{0:T(128)S(1)} %dynamic_slice.60, pred[64]{0:T(512)(128)(4,1)S(1)} %add_compare_fusion.4), kind=kOutput, calls=%fused_computation.5.clone.1 | convolution fusion | flops 283123712 | bytes 33554752 | tf_op jit(solution)/shard_map/while/body/eval_jaxpr/dot_general | solution.py:46
  116.9 2.9 fusion.73
  119.8 4.7 copy.22
  125.9 6.7 %fusion.75 = f32[64,32768]{1,0:T(8,128)} fusion(f32[64,32768]{1,0:T(8,128)S(1)} %fusion.74, f32[64,32768]{1,0:T(8,128)} %get-tuple-element.504, f32[64,32768]{1,0:T(8,128)S(1)} %bitcast.50, pred[]{:T(512)S(6)} %compare.6, s32[64]{0:T(128)S(1)} %dynamic_slice.60, pred[64]{0:T(512)(128)(4,1)S(1)} %add_compare_fusion.4), kind=kOutput, calls=%fused_computation.5.clone.1 | convolution fusion | flops 283123712 | bytes 33554752 | tf_op jit(solution)/shard_map/while/body/eval_jaxpr/dot_general | solution.py:46
  135.7 2.9 fusion.73
  138.6 4.7 copy.22
  144.7 6.7 %fusion.75 = f32[64,32768]{1,0:T(8,128)} fusion(f32[64,32768]{1,0:T(8,128)S(1)} %fusion.74, f32[64,32768]{1,0:T(8,128)} %get-tuple-element.504, f32[64,32768]{1,0:T(8,128)S(1)} %bitcast.50, pred[]{:T(512)S(6)} %compare.6, s32[64]{0:T(128)S(1)} %dynamic_slice.60, pred[64]{0:T(512)(128)(4,1)S(1)} %add_compare_fusion.4), kind=kOutput, calls=%fused_computation.5.clone.1 | convolution fusion | flops 283123712 | bytes 33554752 | tf_op jit(solution)/shard_map/while/body/eval_jaxpr/dot_general | solution.py:46
  154.6 2.9 fusion.73
  157.4 4.7 copy.22
  163.5 6.7 %fusion.75 = f32[64,32768]{1,0:T(8,128)} fusion(f32[64,32768]{1,0:T(8,128)S(1)} %fusion.74, f32[64,32768]{1,0:T(8,128)} %get-tuple-element.504, f32[64,32768]{1,0:T(8,128)S(1)} %bitcast.50, pred[]{:T(512)S(6)} %compare.6, s32[64]{0:T(128)S(1)} %dynamic_slice.60, pred[64]{0:T(512)(128)(4,1)S(1)} %add_compare_fusion.4), kind=kOutput, calls=%fused_computation.5.clone.1 | convolution fusion | flops 283123712 | bytes 33554752 | tf_op jit(solution)/shard_map/while/body/eval_jaxpr/dot_general | solution.py:46
  173.4 2.9 fusion.73
  176.3 4.7 copy.22
  182.4 6.7 %fusion.75 = f32[64,32768]{1,0:T(8,128)} fusion(f32[64,32768]{1,0:T(8,128)S(1)} %fusion.74, f32[64,32768]{1,0:T(8,128)} %get-tuple-element.504, f32[64,32768]{1,0:T(8,128)S(1)} %bitcast.50, pred[]{:T(512)S(6)} %compare.6, s32[64]{0:T(128)S(1)} %dynamic_slice.60, pred[64]{0:T(512)(128)(4,1)S(1)} %add_compare_fusion.4), kind=kOutput, calls=%fused_computation.5.clone.1 | convolution fusion | flops 283123712 | bytes 33554752 | tf_op jit(solution)/shard_map/while/body/eval_jaxpr/dot_general | solution.py:46
  189.0 5.8 %convert_element_type.95 = bf16[64,32768]{1,0:T(8,128)(2,1)} convert(f32[64,32768]{1,0:T(8,128)} %get-tuple-element.311) | non-fusion elementwise | flops 2097152 | bytes 12582912 | tf_op jit(solution)/shard_map/convert_element_type | solution.py:96
  194.8 7.4 %convert_element_type.96 = bf16[8192,256]{1,0:T(8,128)(2,1)} reshape(bf16[64,32768]{1,0:T(8,128)(2,1)} %convert_element_type.95) | data formatting | bytes 8388608 | tf_op jit(solution)/shard_map/convert_element_type | solution.py:96
  202.3 77.9 %reduce-scatter.3.cloned.1.call-done = bf16[512,256]{1,0:T(8,128)(2,1)} async-done(((bf16[8192,256]{1,0:T(8,128)(2,1)}), bf16[512,256]{1,0:T(8,128)(2,1)}) %reduce-scatter.3.cloned.1.call-update) | async-done | bytes 262160 | tf_op jit(solution)/shard_map/reduce_scatter | solution.py:95
  283.3 22.5 %copy.10 = bf16[1,1,512,128,128]{3,4,2,1,0:T(8,128)(2,1)} copy(bf16[1,1,512,128,128]{4,3,2,1,0:T(8,128)(2,1)} %bitcast.58) | data formatting | bytes 33554432 | tf_op args[0]
  307.0 27.2 %all-gather.5.cloned.1.call-done = bf16[8192,256]{1,0:T(8,128)(2,1)} async-done(((bf16[512,256]{1,0:T(8,128)(2,1)}), bf16[8192,256]{1,0:T(8,128)(2,1)}) %all-gather.5.cloned.1.call-update) | async-done | bytes 4194320 | tf_op jit(solution)/shard_map/all_gather | solution.py:102
  334.2 7.4 %reshape_reshape.9 = bf16[64,32768]{1,0:T(8,128)(2,1)} reshape(bf16[8192,256]{1,0:T(8,128)(2,1)} %all-gather.5.cloned.1.call-done) | data formatting | bytes 8388608 | tf_op jit(solution)/shard_map/reshape;reshape | solution.py:22
  341.6 157.8 %while.29 = (s32[]{:T(128)}, f32[32,32768]{1,0:T(8,128)}, s32[512]{0:T(512)S(1)}, s32[]{:T(128)}, bf16[512,128,128]{1,2,0:T(8,128)(2,1)}, /*index=5*/s32[512]{0:...) while((s32[]{:T(128)}, f32[32,32768]{1,0:T(8,128)}, ...), condition=%wide.region_5.0_spmd.clone, body=%wide.region_4.0_spmd.clone.sunk | while | flops 1089482880 | bytes 115345592 | solution.py:52
  342.4 3.5 convolution_convert_fusion.6
  347.0 2.9 fusion.82
  349.9 4.7 copy.24
  362.2 3.5 convolution_convert_fusion.6
  366.8 2.9 fusion.82
  369.6 4.7 copy.24
  376.5 2.6 fusion.84
  381.9 3.5 convolution_convert_fusion.6
  386.5 2.9 fusion.82
  389.3 4.7 copy.24
  396.3 2.6 fusion.84
  401.6 3.5 convolution_convert_fusion.6
  406.2 2.9 fusion.82
  409.0 4.7 copy.24
  416.0 2.6 fusion.84
  421.3 3.5 convolution_convert_fusion.6
  425.9 2.9 fusion.82
  428.8 4.7 copy.24
  441.0 3.5 convolution_convert_fusion.6
  445.6 2.9 fusion.82
  448.5 4.7 copy.24
  455.4 2.6 fusion.84
  460.8 3.5 convolution_convert_fusion.6
  465.4 2.9 fusion.82
  468.2 4.7 copy.24
  475.1 2.6 fusion.84
  480.5 3.5 convolution_convert_fusion.6
  485.1 2.9 fusion.82
  487.9 4.7 copy.24
  505.9 32.0 %reduce-scatter.5.cloned.1.call-done = bf16[512,256]{1,0:T(8,128)(2,1)} async-done(((bf16[4096,256]{1,0:T(8,128)(2,1)}), bf16[512,256]{1,0:T(8,128)(2,1)}) %reduce-scatter.5.cloned.1.call-update) | async-done | bytes 262160 | tf_op jit(solution)/shard_map/reduce_scatter | solution.py:119
  (155 shorter events, 105.9 us)
Async XLA Ops:
  7.2 273.0 %copy-start = (bf16[256,256]{1,0:T(8,128)(2,1)S(1)}, bf16[256,256]{1,0:T(8,128)(2,1)}, u32[]{:S(2)}) copy-start(bf16[256,256]{1,0:T(8,128)(2,1)} %param.16) | copy-start | bytes 393220
  7.2 33.3 %copy-start.7 = (s32[1,1,512]{2,1,0:T(1,128)S(1)}, s32[1,1,512]{2,1,0:T(1,128)}, u32[]{:S(2)}) copy-start(s32[1,1,512]{2,1,0:T(1,128)} %param.13) | copy-start | bytes 6148
  7.2 33.3 %copy-start.6 = (s32[1,1,512]{2,1,0:T(1,128)S(1)}, s32[1,1,512]{2,1,0:T(1,128)}, u32[]{:S(2)}) copy-start(s32[1,1,512]{2,1,0:T(1,128)} %param.12) | copy-start | bytes 6148
  7.2 30.4 %all-gather.3.cloned.1.call-start = ((), (), s32[]{:S(2)}) async-start(), calls=%async_computation.2 | async-start | bytes 2359296 | tf_op jit(solution)/shard_map/all_gather | solution.py:80
  7.9 272.3 %reduce-scatter.3.cloned.1.call-start = ((), (), s32[]{:S(2)}) async-start(), calls=%async_computation.3 | async-start | bytes 4456448 | tf_op jit(solution)/shard_map/reduce_scatter | solution.py:95
  202.2 78.0 %copy-start.5 = (bf16[512,256]{1,0:T(8,128)(2,1)S(1)}, bf16[512,256]{1,0:T(8,128)(2,1)}, u32[]{:S(2)}) copy-start(bf16[512,256]{1,0:T(8,128)(2,1)} %param.17) | copy-start | bytes 786436
  202.2 132.0 %all-gather.5.cloned.1.call-start = ((), (), s32[]{:S(2)}) async-start(), calls=%async_computation.5 | async-start | bytes 4456448 | tf_op jit(solution)/shard_map/all_gather | solution.py:102
  283.2 221.0 %all-reduce.2.cloned.1.call-start = ((), (), s32[]{:S(2)}) async-start(), calls=%async_computation.4 | async-start | bytes 524288 | tf_op jit(solution)/shard_map/psum | solution.py:106
  283.3 22.5 %copy-start.4 = (bf16[512,256]{1,0:T(8,128)(2,1)S(1)}, bf16[512,256]{1,0:T(8,128)(2,1)}, u32[]{:S(2)}) copy-start(bf16[512,256]{1,0:T(8,128)(2,1)} %reduce-scatter.3.cloned.1.call-done) | copy-start | bytes 786436
  306.8 231.2 %reduce-scatter.5.cloned.1.call-start = ((), (), s32[]{:S(2)}) async-start(), calls=%async_computation.6 | async-start | bytes 2359296 | tf_op jit(solution)/shard_map/reduce_scatter | solution.py:119
  354.6 2.2 copy-start.2
  359.4 2.0 copy-start.3
  374.4 2.2 copy-start.2
  379.1 2.0 copy-start.3
  394.1 2.2 copy-start.2
  398.8 2.0 copy-start.3
  413.8 2.2 copy-start.2
  418.5 2.0 copy-start.3
  433.5 2.2 copy-start.2
  438.2 2.0 copy-start.3
  453.2 2.2 copy-start.2
  458.0 2.0 copy-start.3
  473.0 2.2 copy-start.2
  477.7 2.0 copy-start.3
  492.7 2.2 copy-start.2
  497.4 2.0 copy-start.3
  499.4 40.4 %copy-start.1 = (bf16[256,256]{1,0:T(8,128)(2,1)S(1)}, bf16[256,256]{1,0:T(8,128)(2,1)}, u32[]{:S(2)}) copy-start(bf16[256,256]{1,0:T(8,128)(2,1)} %param.16) | copy-start | bytes 393220
Sparse Core Ops, SparseCore 0:
  9.8 27.8 all-gather.2
  202.3 77.8 reduce-scatter.2
  283.4 50.7 all-gather.4
  340.1 141.5 all-reduce.1
  504.4 33.5 reduce-scatter.4
where the time goes:
time: 549 us; the launch traced here: 546 us
  matrix products  177 us (32%)
  waiting for transfers between devices  168 us (31%)
  local copies, waits for them, and re-layouts  165 us (30%)
  other arithmetic  22 us (4%)
  between operations  13.9 us (3%)
    while x64, local copies, waits for them, and re-layouts  120 us
    reduce_scatter x1, waiting for transfers between devices, per_device(): lax.psum_scatter(partial_flat.astype(jnp.bfloat16), 'col', scatter_dimens...  77.9 us
    dot_general x16, matrix products, add_block(): lax.dot_general(add_table, lower_part, contract, preferred_element_type=j...  71.5 us
    dot_general x16, matrix products, add_block(): jnp.einsum(einsum_form, tile_part, picked, preferred_element_type=jnp.flo...  45.7 us
    dot_general x16, matrix products, add_block(): jnp.dot(take_table, source_flat, preferred_element_type=jnp.float32)  38.1 us
    reduce_scatter x1, waiting for transfers between devices, per_device(): lax.psum_scatter(partial_cols.reshape(col_tiles * tile_edge, feat_width)....  32 us
    all_gather x1, waiting for transfers between devices, per_device(): column_block = lax.all_gather(features, 'row', axis=0, tiled=True)  29.6 us
    all_gather x1, waiting for transfers between devices, per_device(): row_block = lax.all_gather(own_grad, 'col', axis=0, tiled=True)  27.2 us
  transfers between devices with their start and end apart: 5, of which 4 were waited for; matrix products, arithmetic and copies ran while one was open for 31% of the time, Pallas kernels for 0%

commit v1 on v0

--- a/solution.py
+++ b/solution.py
@@ -77,7 +77,12 @@
     col_tiles = row_count * own_rows // tile_edge
     block_size = min(slot_total, 64)
     loop_count = slot_total // block_size
-    column_block = lax.all_gather(features, "row", axis=0, tiled=True)
+    ring = [features]
+    for hop in range(7):
+        ring.append(lax.ppermute(ring[-1], "row", [(dev, (dev + 1) % 8) for dev in range(8)]))
+    column_block = jnp.roll(
+        jnp.concatenate(ring[::-1], axis=0), (lax.axis_index("row") + 1) * ring[0].shape[0], axis=0
+    )
     source = column_block.reshape(col_tiles, tile_edge, feat_width)
     partial_rows = sparse_product(
         tile_block,

time: 549 us -> 570 us (1.038)
  waiting for transfers between devices: 168 us -> 186 us
    ppermute x0 -> x7, waiting for transfers between devices: none -> 49.8 us  [per_device(): lax.ppermute(ring[-1], 'row', [(dev, (dev + 1) % 8) for dev in range(8)])]
    all_gather x1 -> x0, waiting for transfers between devices: 29.6 us -> none  [per_device(): column_block = lax.all_gather(features, 'row', axis=0, tiled=True)]
    unnamed x13 -> x30, local copies, waits for them, and re-layouts: 22.5 us -> 23.8 us
  transfers between devices with their start and end apart: 5 -> 11, of which waited for: 4 -> 10; matrix products, arithmetic and copies ran while one was open for 31% -> 30% of each run, Pallas kernels for 0% -> 0%
where the time goes in v1:
time: 570 us; the launch traced here: 567 us
  waiting for transfers between devices  186 us (33%)
  matrix products  177 us (31%)
  local copies, waits for them, and re-layouts  168 us (29%)
  other arithmetic  22 us (4%)
  between operations  14 us (2%)
    while x64, local copies, waits for them, and re-layouts  120 us
    reduce_scatter x1, waiting for transfers between devices, per_device(): lax.psum_scatter(partial_flat.astype(jnp.bfloat16), 'col', scatter_dimens...  76.4 us
    dot_general x16, matrix products, add_block(): lax.dot_general(add_table, lower_part, contract, preferred_element_type=j...  71.4 us
    ppermute x7, waiting for transfers between devices, per_device(): lax.ppermute(ring[-1], 'row', [(dev, (dev + 1) % 8) for dev in range(8)])  49.8 us
    dot_general x16, matrix products, add_block(): jnp.einsum(einsum_form, tile_part, picked, preferred_element_type=jnp.flo...  45.7 us
    dot_general x16, matrix products, add_block(): jnp.dot(take_table, source_flat, preferred_element_type=jnp.float32)  38.1 us
    reduce_scatter x1, waiting for transfers between devices, per_device(): lax.psum_scatter(partial_cols.reshape(col_tiles * tile_edge, feat_width)....  32.1 us
    all_gather x1, waiting for transfers between devices, per_device(): row_block = lax.all_gather(own_grad, 'col', axis=0, tiled=True)  27.3 us
  transfers between devices with their start and end apart: 11, of which 10 were waited for; matrix products, arithmetic and copies ran while one was open for 30% of the time, Pallas kernels for 0%

profile of v1, /device:TPU:0, one launch (start us, length us, event | category | flops | bytes accessed | tf_op | source)
XLA Modules:
  0.0 567.4 jit_solution(3468895034375769853)
XLA Ops:
  7.3 7.8 %collective-permute-done = bf16[512,256]{1,0:T(8,128)(2,1)S(1)} collective-permute-done((bf16[512,256]{1,0:T(8,128)(2,1)}, bf16[512,256]{1,0:T(8,128)(2,1)S(1)}, u32[]{:S(2)}, u32[]{:S(2)}) %collective-permute-start) | collective-permute-done | bytes 262176 | tf_op jit(solution)/shard_map/ppermute | solution.py:82
  15.1 7.0 %collective-permute-done.1 = bf16[512,256]{1,0:T(8,128)(2,1)S(1)} collective-permute-done((bf16[512,256]{1,0:T(8,128)(2,1)S(1)}, bf16[512,256]{1,0:T(8,128)(2,1)S(1)}, u32[]{:S(2)}, u32[]{:S(2)}) %collective-permute-start.1) | collective-permute-done | bytes 262176 | tf_op jit(solution)/shard_map/ppermute | solution.py:82
  22.1 7.0 %collective-permute-done.2 = bf16[512,256]{1,0:T(8,128)(2,1)S(1)} collective-permute-done((bf16[512,256]{1,0:T(8,128)(2,1)S(1)}, bf16[512,256]{1,0:T(8,128)(2,1)S(1)}, u32[]{:S(2)}, u32[]{:S(2)}) %collective-permute-start.2) | collective-permute-done | bytes 262176 | tf_op jit(solution)/shard_map/ppermute | solution.py:82
  29.1 7.0 %collective-permute-done.3 = bf16[512,256]{1,0:T(8,128)(2,1)S(1)} collective-permute-done((bf16[512,256]{1,0:T(8,128)(2,1)S(1)}, bf16[512,256]{1,0:T(8,128)(2,1)S(1)}, u32[]{:S(2)}, u32[]{:S(2)}) %collective-permute-start.3) | collective-permute-done | bytes 262176 | tf_op jit(solution)/shard_map/ppermute | solution.py:82
  36.1 7.0 %collective-permute-done.4 = bf16[512,256]{1,0:T(8,128)(2,1)S(1)} collective-permute-done((bf16[512,256]{1,0:T(8,128)(2,1)S(1)}, bf16[512,256]{1,0:T(8,128)(2,1)S(1)}, u32[]{:S(2)}, u32[]{:S(2)}) %collective-permute-start.4) | collective-permute-done | bytes 262176 | tf_op jit(solution)/shard_map/ppermute | solution.py:82
  43.1 7.0 %collective-permute-done.5 = bf16[512,256]{1,0:T(8,128)(2,1)S(1)} collective-permute-done((bf16[512,256]{1,0:T(8,128)(2,1)S(1)}, bf16[512,256]{1,0:T(8,128)(2,1)S(1)}, u32[]{:S(2)}, u32[]{:S(2)}) %collective-permute-start.5) | collective-permute-done | bytes 262176 | tf_op jit(solution)/shard_map/ppermute | solution.py:82
  50.1 7.0 %collective-permute-done.6 = bf16[512,256]{1,0:T(8,128)(2,1)S(1)} collective-permute-done((bf16[512,256]{1,0:T(8,128)(2,1)S(1)}, bf16[512,256]{1,0:T(8,128)(2,1)S(1)}, u32[]{:S(2)}, u32[]{:S(2)}) %collective-permute-start.6) | collective-permute-done | bytes 262176 | tf_op jit(solution)/shard_map/ppermute | solution.py:82
  60.1 2.9 reshape_reshape.8
  63.0 148.4 %while.28 = (s32[]{:T(128)}, f32[64,32768]{1,0:T(8,128)}, s32[512]{0:T(512)S(1)}, s32[]{:T(128)}, bf16[512,128,128]{2,1,0:T(8,128)(2,1)}, /*index=5*/s32[512]{0:...) while((s32[]{:T(128)}, f32[64,32768]{1,0:T(8,128)}, ...), condition=%wide.region_1.2_spmd.clone, body=%wide.region_0.1_spmd.clone.sunk | while | flops 1226852480 | bytes 96471168 | solution.py:52
  66.2 2.9 fusion.73
  69.1 4.7 copy.22
  75.2 4.5 fusion.75
  82.8 2.9 fusion.73
  85.7 4.7 copy.22
  91.8 6.6 %fusion.75 = f32[64,32768]{1,0:T(8,128)} fusion(f32[64,32768]{1,0:T(8,128)S(1)} %fusion.74, f32[64,32768]{1,0:T(8,128)} %get-tuple-element.504, f32[64,32768]{1,0:T(8,128)S(1)} %bitcast.50, pred[]{:T(512)S(6)} %compare.7, s32[64]{0:T(128)S(1)} %dynamic_slice.66, pred[64]{0:T(512)(128)(4,1)S(1)} %add_compare_fusion.4), kind=kOutput, calls=%fused_computation.5.clone.1 | convolution fusion | flops 283123712 | bytes 33554752 | tf_op jit(solution)/shard_map/while/body/eval_jaxpr/dot_general | solution.py:46
  101.7 2.9 fusion.73
  104.5 4.7 copy.22
  110.6 6.6 %fusion.75 = f32[64,32768]{1,0:T(8,128)} fusion(f32[64,32768]{1,0:T(8,128)S(1)} %fusion.74, f32[64,32768]{1,0:T(8,128)} %get-tuple-element.504, f32[64,32768]{1,0:T(8,128)S(1)} %bitcast.50, pred[]{:T(512)S(6)} %compare.7, s32[64]{0:T(128)S(1)} %dynamic_slice.66, pred[64]{0:T(512)(128)(4,1)S(1)} %add_compare_fusion.4), kind=kOutput, calls=%fused_computation.5.clone.1 | convolution fusion | flops 283123712 | bytes 33554752 | tf_op jit(solution)/shard_map/while/body/eval_jaxpr/dot_general | solution.py:46
  120.5 2.9 fusion.73
  123.3 4.7 copy.22
  129.4 6.6 %fusion.75 = f32[64,32768]{1,0:T(8,128)} fusion(f32[64,32768]{1,0:T(8,128)S(1)} %fusion.74, f32[64,32768]{1,0:T(8,128)} %get-tuple-element.504, f32[64,32768]{1,0:T(8,128)S(1)} %bitcast.50, pred[]{:T(512)S(6)} %compare.7, s32[64]{0:T(128)S(1)} %dynamic_slice.66, pred[64]{0:T(512)(128)(4,1)S(1)} %add_compare_fusion.4), kind=kOutput, calls=%fused_computation.5.clone.1 | convolution fusion | flops 283123712 | bytes 33554752 | tf_op jit(solution)/shard_map/while/body/eval_jaxpr/dot_general | solution.py:46
  139.3 2.9 fusion.73
  142.1 4.7 copy.22
  148.3 6.6 %fusion.75 = f32[64,32768]{1,0:T(8,128)} fusion(f32[64,32768]{1,0:T(8,128)S(1)} %fusion.74, f32[64,32768]{1,0:T(8,128)} %get-tuple-element.504, f32[64,32768]{1,0:T(8,128)S(1)} %bitcast.50, pred[]{:T(512)S(6)} %compare.7, s32[64]{0:T(128)S(1)} %dynamic_slice.66, pred[64]{0:T(512)(128)(4,1)S(1)} %add_compare_fusion.4), kind=kOutput, calls=%fused_computation.5.clone.1 | convolution fusion | flops 283123712 | bytes 33554752 | tf_op jit(solution)/shard_map/while/body/eval_jaxpr/dot_general | solution.py:46
  158.1 2.9 fusion.73
  161.0 4.7 copy.22
  167.1 6.6 %fusion.75 = f32[64,32768]{1,0:T(8,128)} fusion(f32[64,32768]{1,0:T(8,128)S(1)} %fusion.74, f32[64,32768]{1,0:T(8,128)} %get-tuple-element.504, f32[64,32768]{1,0:T(8,128)S(1)} %bitcast.50, pred[]{:T(512)S(6)} %compare.7, s32[64]{0:T(128)S(1)} %dynamic_slice.66, pred[64]{0:T(512)(128)(4,1)S(1)} %add_compare_fusion.4), kind=kOutput, calls=%fused_computation.5.clone.1 | convolution fusion | flops 283123712 | bytes 33554752 | tf_op jit(solution)/shard_map/while/body/eval_jaxpr/dot_general | solution.py:46
  176.9 2.9 fusion.73
  179.8 4.7 copy.22
  185.9 6.6 %fusion.75 = f32[64,32768]{1,0:T(8,128)} fusion(f32[64,32768]{1,0:T(8,128)S(1)} %fusion.74, f32[64,32768]{1,0:T(8,128)} %get-tuple-element.504, f32[64,32768]{1,0:T(8,128)S(1)} %bitcast.50, pred[]{:T(512)S(6)} %compare.7, s32[64]{0:T(128)S(1)} %dynamic_slice.66, pred[64]{0:T(512)(128)(4,1)S(1)} %add_compare_fusion.4), kind=kOutput, calls=%fused_computation.5.clone.1 | convolution fusion | flops 283123712 | bytes 33554752 | tf_op jit(solution)/shard_map/while/body/eval_jaxpr/dot_general | solution.py:46
  195.7 2.9 fusion.73
  198.6 4.7 copy.22
  204.7 6.6 %fusion.75 = f32[64,32768]{1,0:T(8,128)} fusion(f32[64,32768]{1,0:T(8,128)S(1)} %fusion.74, f32[64,32768]{1,0:T(8,128)} %get-tuple-element.504, f32[64,32768]{1,0:T(8,128)S(1)} %bitcast.50, pred[]{:T(512)S(6)} %compare.7, s32[64]{0:T(128)S(1)} %dynamic_slice.66, pred[64]{0:T(512)(128)(4,1)S(1)} %add_compare_fusion.4), kind=kOutput, calls=%fused_computation.5.clone.1 | convolution fusion | flops 283123712 | bytes 33554752 | tf_op jit(solution)/shard_map/while/body/eval_jaxpr/dot_general | solution.py:46
  211.3 5.8 %convert_element_type.95 = bf16[64,32768]{1,0:T(8,128)(2,1)} convert(f32[64,32768]{1,0:T(8,128)} %get-tuple-element.311) | non-fusion elementwise | flops 2097152 | bytes 12582912 | tf_op jit(solution)/shard_map/convert_element_type | solution.py:101
  217.1 7.4 %convert_element_type.96 = bf16[8192,256]{1,0:T(8,128)(2,1)} reshape(bf16[64,32768]{1,0:T(8,128)(2,1)} %convert_element_type.95) | data formatting | bytes 8388608 | tf_op jit(solution)/shard_map/convert_element_type | solution.py:101
  224.7 76.4 %reduce-scatter.3.cloned.1.call-done = bf16[512,256]{1,0:T(8,128)(2,1)} async-done(((bf16[8192,256]{1,0:T(8,128)(2,1)}), bf16[512,256]{1,0:T(8,128)(2,1)}) %reduce-scatter.3.cloned.1.call-update) | async-done | bytes 262160 | tf_op jit(solution)/shard_map/reduce_scatter | solution.py:100
  304.2 22.5 %copy.10 = bf16[1,1,512,128,128]{3,4,2,1,0:T(8,128)(2,1)} copy(bf16[1,1,512,128,128]{4,3,2,1,0:T(8,128)(2,1)} %bitcast.58) | data formatting | bytes 33554432 | tf_op args[0]
  327.8 27.3 %all-gather.2.cloned.1.call-done = bf16[8192,256]{1,0:T(8,128)(2,1)} async-done(((bf16[512,256]{1,0:T(8,128)(2,1)}), bf16[8192,256]{1,0:T(8,128)(2,1)}) %all-gather.2.cloned.1.call-update) | async-done | bytes 4194320 | tf_op jit(solution)/shard_map/all_gather | solution.py:107
  355.1 7.4 %reshape_reshape.9 = bf16[64,32768]{1,0:T(8,128)(2,1)} reshape(bf16[8192,256]{1,0:T(8,128)(2,1)} %all-gather.2.cloned.1.call-done) | data formatting | bytes 8388608 | tf_op jit(solution)/shard_map/reshape;reshape | solution.py:22
  362.5 158.0 %while.29 = (s32[]{:T(128)}, f32[32,32768]{1,0:T(8,128)}, s32[512]{0:T(512)S(1)}, s32[]{:T(128)}, bf16[512,128,128]{1,2,0:T(8,128)(2,1)}, /*index=5*/s32[512]{0:...) while((s32[]{:T(128)}, f32[32,32768]{1,0:T(8,128)}, ...), condition=%wide.region_5.6_spmd.clone, body=%wide.region_4.5_spmd.clone.sunk | while | flops 1089482880 | bytes 115345592 | solution.py:52
  363.3 3.5 convolution_convert_fusion.6
  367.9 2.9 fusion.82
  370.7 4.7 copy.24
  383.1 3.5 convolution_convert_fusion.6
  387.7 2.9 fusion.82
  390.5 4.7 copy.24
  402.8 3.5 convolution_convert_fusion.6
  407.4 2.9 fusion.82
  410.3 4.7 copy.24
  422.6 3.5 convolution_convert_fusion.6
  430.0 4.7 copy.24
  442.3 3.5 convolution_convert_fusion.6
  446.9 2.9 fusion.82
  449.8 4.7 copy.24
  462.1 3.5 convolution_convert_fusion.6
  466.6 2.9 fusion.82
  469.5 4.7 copy.24
  481.8 3.5 convolution_convert_fusion.6
  486.4 2.9 fusion.82
  489.3 4.7 copy.24
  501.6 3.5 convolution_convert_fusion.6
  506.1 2.9 fusion.82
  509.0 4.7 copy.24
  527.0 32.1 %reduce-scatter.5.cloned.1.call-done = bf16[512,256]{1,0:T(8,128)(2,1)} async-done(((bf16[4096,256]{1,0:T(8,128)(2,1)}), bf16[512,256]{1,0:T(8,128)(2,1)}) %reduce-scatter.5.cloned.1.call-update) | async-done | bytes 262160 | tf_op jit(solution)/shard_map/reduce_scatter | solution.py:124
  (185 shorter events, 123.8 us)
Async XLA Ops:
  7.2 294.0 %copy-start = (bf16[256,256]{1,0:T(8,128)(2,1)S(1)}, bf16[256,256]{1,0:T(8,128)(2,1)}, u32[]{:S(2)}) copy-start(bf16[256,256]{1,0:T(8,128)(2,1)} %param.16) | copy-start | bytes 393220
  7.2 51.3 %copy-start.4 = (bf16[512,256]{1,0:T(8,128)(2,1)S(1)}, bf16[512,256]{1,0:T(8,128)(2,1)}, u32[]{:S(2)}) copy-start(bf16[512,256]{1,0:T(8,128)(2,1)} %param.15) | copy-start | bytes 786436
  7.2 293.9 %reduce-scatter.3.cloned.1.call-start = ((), (), s32[]{:S(2)}) async-start(), calls=%async_computation.2 | async-start | bytes 4456448 | tf_op jit(solution)/shard_map/reduce_scatter | solution.py:100
  7.2 7.8 %collective-permute-start = (bf16[512,256]{1,0:T(8,128)(2,1)}, bf16[512,256]{1,0:T(8,128)(2,1)S(1)}, u32[]{:S(2)}, u32[]{:S(2)}) collective-permute-start(bf16[512,256]{1,0:T(8,128)(2,1)} %param.15), channel_id=1, source_target_pairs={{0,16},{16,32},{32,48},{48,64},{64,80},{80,96},{96,112},{112,0},{1... | collective-permute-start | bytes 786440 | tf_op jit(solution)/shard_map/ppermute | solution.py:82
  15.1 7.0 %collective-permute-start.1 = (bf16[512,256]{1,0:T(8,128)(2,1)S(1)}, bf16[512,256]{1,0:T(8,128)(2,1)S(1)}, u32[]{:S(2)}, u32[]{:S(2)}) collective-permute-start(bf16[512,256]{1,0:T(8,128)(2,1)S(1)} %collective-permute-done), channel_id=1, source_target_pairs={{0,16},{16,32},{32,48},{48,64},{64,80},{80,96},{96,112},{112,0},{1... | collective-permute-start | bytes 786440 | tf_op jit(solution)/shard_map/ppermute | solution.py:82
  22.1 7.0 %collective-permute-start.2 = (bf16[512,256]{1,0:T(8,128)(2,1)S(1)}, bf16[512,256]{1,0:T(8,128)(2,1)S(1)}, u32[]{:S(2)}, u32[]{:S(2)}) collective-permute-start(bf16[512,256]{1,0:T(8,128)(2,1)S(1)} %collective-permute-done.1), channel_id=1, source_target_pairs={{0,16},{16,32},{32,48},{48,64},{64,80},{80,96},{96,112},{112,0},{1... | collective-permute-start | bytes 786440 | tf_op jit(solution)/shard_map/ppermute | solution.py:82
  29.1 7.0 %collective-permute-start.3 = (bf16[512,256]{1,0:T(8,128)(2,1)S(1)}, bf16[512,256]{1,0:T(8,128)(2,1)S(1)}, u32[]{:S(2)}, u32[]{:S(2)}) collective-permute-start(bf16[512,256]{1,0:T(8,128)(2,1)S(1)} %collective-permute-done.2), channel_id=1, source_target_pairs={{0,16},{16,32},{32,48},{48,64},{64,80},{80,96},{96,112},{112,0},{1... | collective-permute-start | bytes 786440 | tf_op jit(solution)/shard_map/ppermute | solution.py:82
  36.1 7.0 %collective-permute-start.4 = (bf16[512,256]{1,0:T(8,128)(2,1)S(1)}, bf16[512,256]{1,0:T(8,128)(2,1)S(1)}, u32[]{:S(2)}, u32[]{:S(2)}) collective-permute-start(bf16[512,256]{1,0:T(8,128)(2,1)S(1)} %collective-permute-done.3), channel_id=1, source_target_pairs={{0,16},{16,32},{32,48},{48,64},{64,80},{80,96},{96,112},{112,0},{1... | collective-permute-start | bytes 786440 | tf_op jit(solution)/shard_map/ppermute | solution.py:82
  43.1 7.0 %collective-permute-start.5 = (bf16[512,256]{1,0:T(8,128)(2,1)S(1)}, bf16[512,256]{1,0:T(8,128)(2,1)S(1)}, u32[]{:S(2)}, u32[]{:S(2)}) collective-permute-start(bf16[512,256]{1,0:T(8,128)(2,1)S(1)} %collective-permute-done.4), channel_id=1, source_target_pairs={{0,16},{16,32},{32,48},{48,64},{64,80},{80,96},{96,112},{112,0},{1... | collective-permute-start | bytes 786440 | tf_op jit(solution)/shard_map/ppermute | solution.py:82
  50.1 7.0 %collective-permute-start.6 = (bf16[512,256]{1,0:T(8,128)(2,1)S(1)}, bf16[512,256]{1,0:T(8,128)(2,1)S(1)}, u32[]{:S(2)}, u32[]{:S(2)}) collective-permute-start(bf16[512,256]{1,0:T(8,128)(2,1)S(1)} %collective-permute-done.5), channel_id=1, source_target_pairs={{0,16},{16,32},{32,48},{48,64},{64,80},{80,96},{96,112},{112,0},{1... | collective-permute-start | bytes 786440 | tf_op jit(solution)/shard_map/ppermute | solution.py:82
  58.5 4.4 copy-start.7
  58.5 4.4 copy-start.8
  224.5 76.7 %copy-start.6 = (bf16[512,256]{1,0:T(8,128)(2,1)S(1)}, bf16[512,256]{1,0:T(8,128)(2,1)}, u32[]{:S(2)}) copy-start(bf16[512,256]{1,0:T(8,128)(2,1)} %param.17) | copy-start | bytes 786436
  224.5 130.6 %all-gather.2.cloned.1.call-start = ((), (), s32[]{:S(2)}) async-start(), calls=%async_computation.4 | async-start | bytes 4456448 | tf_op jit(solution)/shard_map/all_gather | solution.py:107
  304.2 221.2 %all-reduce.2.cloned.1.call-start = ((), (), s32[]{:S(2)}) async-start(), calls=%async_computation.3 | async-start | bytes 524288 | tf_op jit(solution)/shard_map/psum | solution.py:111
  304.2 22.5 %copy-start.5 = (bf16[512,256]{1,0:T(8,128)(2,1)S(1)}, bf16[512,256]{1,0:T(8,128)(2,1)}, u32[]{:S(2)}) copy-start(bf16[512,256]{1,0:T(8,128)(2,1)} %reduce-scatter.3.cloned.1.call-done) | copy-start | bytes 786436
  327.7 231.4 %reduce-scatter.5.cloned.1.call-start = ((), (), s32[]{:S(2)}) async-start(), calls=%async_computation.5 | async-start | bytes 2359296 | tf_op jit(solution)/shard_map/reduce_scatter | solution.py:124
  375.5 2.2 copy-start.2
  380.3 2.0 copy-start.3
  395.3 2.2 copy-start.2
  400.0 2.0 copy-start.3
  415.0 2.2 copy-start.2
  419.8 2.0 copy-start.3
  434.8 2.2 copy-start.2
  439.5 2.0 copy-start.3
  454.5 2.2 copy-start.2
  459.3 2.0 copy-start.3
  474.2 2.2 copy-start.2
  479.0 2.0 copy-start.3
  494.0 2.2 copy-start.2
  498.8 2.0 copy-start.3
  513.7 2.2 copy-start.2
  518.5 2.0 copy-start.3
  520.5 40.4 %copy-start.1 = (bf16[256,256]{1,0:T(8,128)(2,1)S(1)}, bf16[256,256]{1,0:T(8,128)(2,1)}, u32[]{:S(2)}) copy-start(bf16[256,256]{1,0:T(8,128)(2,1)} %param.16) | copy-start | bytes 393220
Sparse Core Ops, SparseCore 0:
  224.6 76.4 reduce-scatter.2
  304.3 50.7 all-gather.1
  361.2 141.5 all-reduce.1
  525.5 33.6 reduce-scatter.4
